TPU v7x, 32 devices: a whole 2x2x4 slice. The times are simulated.
32 devices in a mesh: region: 8 (over z, y), member: 4 (over x, core).
Axes of the slice: x: 2, y: 2, z: 4, core: 2. Of those that a mesh axis runs over, the one named last changes fastest.
Arguments:
- ensemble: bfloat16 [256, 16384], P('member', 'region'), may hold values from -6 to 6
- reports: float32 [8, 1024], P('region'), may hold values from -6 to 6
- report_count: int32 [8], P('region'), may hold values from 128 to 1024, as said below
- report_cell: int32 [8, 1024], P('region'), may hold values from 0 to 16383, as said below
- report_weight: float32 [8, 16, 1024], P('region', 'member'), may hold values from 0.001 to 1
- blending: float32 [4, 16384], P(None, ('region', 'member')), may hold values from 0.02 to 1
Outputs:
- analysis: bfloat16 [16384, 256], P(('region', 'member'))
Inputs may be any that keep to these rules, and one draw needn't show every extreme that they name: `report_count`: the largest value 1024 is reached by some region in every draw. `report_cell`: every cell lies in the slot's own region, or in the first 128 cells of one of at most two other regions chosen for that region.
All inputs are finite; a program needn't handle non-finite values.
Results may differ from a plain program's by a relative error of at most 0.0055.
Values may be sent and summed in bfloat16 or wider, within the bound.
No kernel may reach another device: no remote copies, remote signals or barrier semaphores. Data moves between devices by JAX's collectives and lax.ppermute only.
A program may use at most 64 MiB of HBM per device.

v0:
```python
import jax
import jax.numpy as jnp
from jax import lax
from jax.sharding import PartitionSpec as P

MARGIN = 128
SWEEPS = 4
highest = lax.Precision.HIGHEST


def extended(block, sides, width):
    for axis, dim in sides:
        count = lax.axis_size(axis)
        forward = [(i, i + 1) for i in range(count - 1)]
        backward = [(target, source) for source, target in forward]
        low = lax.ppermute(
            lax.slice_in_dim(block, block.shape[dim] - width, None, axis=dim), axis, forward
        )
        high = lax.ppermute(lax.slice_in_dim(block, 0, width, axis=dim), axis, backward)
        block = jnp.concatenate([low, block, high], axis=dim)
    return block


def make_transform(products, forcing, members):
    identity = jnp.eye(members, dtype=jnp.float32)
    precision_mat = (members - 1.0) * identity[None] + products
    frobenius = jnp.sqrt(jnp.sum(precision_mat * precision_mat, axis=(1, 2)))
    current = precision_mat / frobenius[:, None, None]
    root_iter = jnp.broadcast_to(identity, current.shape)
    for iteration in range(SWEEPS):
        middle = 1.5 * identity[None] - 0.5 * jnp.einsum(
            "aij,ajk->aik", root_iter, current, precision=highest
        )
        current = jnp.einsum("aij,ajk->aik", current, middle, precision=highest)
        root_iter = jnp.einsum("aij,ajk->aik", middle, root_iter, precision=highest)
    inverse_root = root_iter / jnp.sqrt(frobenius)[:, None, None]
    inner_step = jnp.einsum("aij,aj->ai", inverse_root, forcing, precision=highest)
    mean_weights = jnp.einsum("aij,aj->ai", inverse_root, inner_step, precision=highest)
    return (mean_weights[:, :, None] + jnp.sqrt(members - 1.0) * inverse_root).astype(jnp.bfloat16)


def corner_layout(band_index, points_here, row_count):
    group_index = jnp.arange(4 * points_here, dtype=jnp.int32)
    upper_half = group_index // (2 * points_here)
    column_block = group_index // 2 % points_here
    right_half = group_index % 2
    row_base = jnp.clip(band_index - 1 + upper_half, 0, row_count - 2)
    col_base = jnp.clip(column_block - 1 + right_half, 0, points_here - 2)
    return (row_base, col_base)


def per_device(ensemble, reports, report_count, report_cell, report_weight, blending):
    local_members, cell_count = ensemble.shape
    groups = lax.axis_size("member")
    members = local_members * groups
    region = lax.axis_index("region")
    member = lax.axis_index("member")
    targets = report_cell[0]
    holder = targets // cell_count
    within = targets % cell_count
    is_local = holder == region
    local_values = jnp.take(ensemble, jnp.where(is_local, within, 0), axis=1).astype(jnp.float32)
    border = ensemble[:, :MARGIN]
    border_index = holder * MARGIN + jnp.minimum(within, MARGIN - 1)
    pieces = lax.all_gather(border, "region", axis=1, tiled=True)
    extent = pieces.shape[1]
    inside = (border_index >= 0) & (border_index < extent) & jnp.logical_not(is_local)
    picked = jnp.take(pieces, jnp.clip(border_index, 0, extent - 1), axis=1).astype(jnp.float32)
    remote = jnp.where(inside[None, :], picked, 0.0)
    at_reports = jnp.where(is_local[None, :], local_values, remote)
    report_mean = lax.psum(jnp.sum(at_reports, axis=0), "member") / members
    local_pert = (at_reports - report_mean[None, :]).astype(jnp.bfloat16)
    report_pert = lax.all_gather(local_pert, "member", axis=0, tiled=True)
    active = (jnp.arange(report_pert.shape[1]) < report_count[0]).astype(jnp.float32)
    weights = report_weight[0] * active[None, :]
    weighted = (report_pert[None, :, :] * weights[:, None, :]).astype(jnp.bfloat16)
    departure = (weights * (reports[0] - report_mean)[None, :]).astype(jnp.bfloat16)
    products = jnp.einsum("ako,jo->akj", weighted, report_pert, preferred_element_type=jnp.float32)
    forcing = jnp.einsum("ao,ko->ak", departure, report_pert, preferred_element_type=jnp.float32)
    transform = make_transform(products, forcing, members)
    points_here = transform.shape[0]
    groups_band = 4 * points_here
    slab_cells = cell_count // groups
    group_cells = slab_cells // groups_band
    mixing = blending / jnp.sum(blending, axis=0, keepdims=True)
    columns = lax.all_to_all(ensemble, "member", split_axis=1, concat_axis=0, tiled=True)
    cell_mean = jnp.sum(columns, axis=0, dtype=jnp.float32) / members
    anomaly = (columns - cell_mean[None, :]).astype(jnp.bfloat16)
    anomaly_view = anomaly.reshape(members, groups_band, group_cells)
    mix_view = mixing.reshape(4, groups_band, group_cells)
    neighbours = extended(transform[None], (("member", 0),), 1)
    stacked = neighbours.reshape(3 * points_here, members, members)
    row_base, col_base = corner_layout(member, points_here, groups)
    running = jnp.zeros((groups_band, group_cells, members), jnp.float32)
    for corner in range(4):
        row_step = corner // 2
        col_step = corner % 2
        chosen_index = (row_base + row_step - (member - 1)) * points_here + col_base + col_step
        chosen = jnp.take(stacked, chosen_index, axis=0)
        spread = jnp.einsum(
            "kgc,gkj->gcj", anomaly_view, chosen, preferred_element_type=jnp.float32
        )
        running = running + mix_view[corner][:, :, None] * spread
    blended = running.reshape(slab_cells, members)
    return (cell_mean[:, None] + blended).astype(jnp.bfloat16)


def solution(mesh):
    return jax.shard_map(
        per_device,
        mesh=mesh,
        in_specs=(
            P("member", "region"),
            P("region", None),
            P("region"),
            P("region", None),
            P("region", "member", None),
            P(None, ("region", "member")),
        ),
        out_specs=P(("region", "member"), None),
        check_vma=False,
    )
```

profile of v0, /device:TPU:0, one launch (start us, length us, event | category | flops | bytes accessed | tf_op | source)
XLA Modules:
  0.0 104.7 jit_solution(4873198254214473473)
XLA Ops:
  0.0 0.8 compare_select_fusion
  1.6 1.2 %copy.24 = bf16[64,2048]{0,1:T(8,128)(2,1)S(1)} copy(bf16[64,2048]{1,0:T(8,128)(2,1)} %param.8) | data formatting | bytes 524288 | tf_op args[0]
  2.9 3.2 %gather_fusion = bf16[1024,64]{1,0:T(8,128)(2,1)S(1)} fusion(bf16[64,2048]{0,1:T(8,128)(2,1)S(1)} %copy.24, s32[1024]{0:T(1024)S(1)} %broadcast_clamp_fusion.1), kind=kCustom, calls=%fused_computation.4 | custom fusion | bytes 266240 | tf_op jit(solution)/shard_map/jit(_take)/gather | solution.py:62
  6.3 32.6 %all_gather.6 = bf16[64,1024]{0,1:T(8,128)(2,1)S(1)} all-gather(bf16[64,128]{0,1:T(8,128)(2,1)S(1)} %slice.37), channel_id=1, replica_groups=mesh['region'=8,'member'=4] {'region'}, dimensions={1}, use_global_device_ids=true | all-gather | bytes 147456 | tf_op jit(solution)/shard_map/all_gather | solution.py:65
  38.9 3.2 %gather_fusion.1 = bf16[1024,64]{1,0:T(8,128)(2,1)S(1)} fusion(bf16[64,1024]{0,1:T(8,128)(2,1)S(1)} %all_gather.6, s32[1024]{0:T(1024)S(1)} %broadcast_clamp_fusion), kind=kCustom, calls=%fused_computation.5 | custom fusion | bytes 266240 | tf_op jit(solution)/shard_map/jit(_take)/gather | solution.py:68
  42.3 5.7 %psum.7 = f32[1024]{0:T(1024)S(1)} all-reduce(f32[1024]{0:T(1024)S(1)} %fusion.54), channel_id=1, replica_groups=mesh['region'=8,'member'=4] {'member'}, use_global_device_ids=true, to_apply=%region_3.4 | all-reduce | flops 1024 | bytes 8192 | tf_op jit(solution)/shard_map/psum | solution.py:71
  48.1 7.4 %all_gather.7 = bf16[256,1024]{1,0:T(8,128)(2,1)S(1)} all-gather(bf16[64,1024]{1,0:T(8,128)(2,1)S(1)} %fusion.56), channel_id=1, replica_groups=mesh['region'=8,'member'=4] {'member'}, dimensions={0}, use_global_device_ids=true | all-gather | bytes 655360 | tf_op jit(solution)/shard_map/all_gather | solution.py:73
  56.3 0.9 multiply_reduce_fusion
  57.2 1.2 %fusion.19 = f32[4,256,256]{2,1,0:T(8,128)S(1)} fusion(f32[256,256]{1,0:T(8,128)S(1)} %fusion.52, f32[256,256]{1,0:T(8,128)S(1)} %fusion.53, f32[4,256,256]{2,1,0:T(8,128)S(1)} %get-tuple-element.24, f32[4]{0:T(128)S(1)} %get-tuple-element.22), kind=kOutput, calls=%fused_computation.32 | convolution fusion | flops 806092800 | bytes 2621456 | tf_op jit(solution)/shard_map/aij,ajk->aik/dot_general | solution.py:31
  58.4 1.2 %fusion.55 = f32[4,256,256]{2,1,0:T(8,128)S(1)} fusion(f32[4,256,256]{2,1,0:T(8,128)S(1)} %fusion.19, f32[4,256,256]{2,1,0:T(8,128)S(1)} %get-tuple-element.24, f32[4]{0:T(128)S(1)} %get-tuple-element.22), kind=kOutput, calls=%fused_computation.66 | convolution fusion | flops 805568512 | bytes 3145744 | tf_op jit(solution)/shard_map/aij,ajk->aik/dot_general | solution.py:34
  59.6 1.1 %fusion.48 = f32[4,256,256]{2,1,0:T(8,128)S(1)} fusion(f32[4,256,256]{2,1,0:T(8,128)S(1)} %fusion.19, f32[256,256]{1,0:T(8,128)S(1)} %fusion.52), kind=kOutput, calls=%fused_computation.54 | convolution fusion | flops 805306368 | bytes 2359296 | tf_op jit(solution)/shard_map/aij,ajk->aik/dot_general | solution.py:35
  60.7 1.2 %fusion.18 = f32[4,256,256]{2,1,0:T(8,128)S(1)} fusion(f32[4,256,256]{2,1,0:T(8,128)S(1)} %fusion.48, f32[4,256,256]{2,1,0:T(8,128)S(1)} %fusion.55, f32[256,256]{1,0:T(8,128)S(1)} %fusion.53), kind=kOutput, calls=%fused_computation.30 | convolution fusion | flops 805830656 | bytes 3407872 | tf_op jit(solution)/shard_map/aij,ajk->aik/dot_general | solution.py:31
  61.9 1.1 %fusion.79 = f32[4,256,256]{2,1,0:T(8,128)S(1)} fusion(f32[4,256,256]{2,1,0:T(8,128)S(1)} %fusion.55, f32[4,256,256]{2,1,0:T(8,128)S(1)} %fusion.18), kind=kOutput, calls=%fused_computation.158 | convolution fusion | flops 805306368 | bytes 3145728 | tf_op jit(solution)/shard_map/aij,ajk->aik/dot_general | solution.py:34
  63.0 1.1 %fusion.78 = f32[4,256,256]{2,1,0:T(8,128)S(1)} fusion(f32[4,256,256]{2,1,0:T(8,128)S(1)} %fusion.18, f32[4,256,256]{2,1,0:T(8,128)S(1)} %fusion.48), kind=kOutput, calls=%fused_computation.157 | convolution fusion | flops 805306368 | bytes 3145728 | tf_op jit(solution)/shard_map/aij,ajk->aik/dot_general | solution.py:35
  64.2 1.2 %fusion.17 = f32[4,256,256]{2,1,0:T(8,128)S(1)} fusion(f32[4,256,256]{2,1,0:T(8,128)S(1)} %fusion.78, f32[4,256,256]{2,1,0:T(8,128)S(1)} %fusion.79, f32[256,256]{1,0:T(8,128)S(1)} %fusion.53), kind=kOutput, calls=%fused_computation.28 | convolution fusion | flops 805830656 | bytes 3407872 | tf_op jit(solution)/shard_map/aij,ajk->aik/dot_general | solution.py:31
  65.4 1.1 %fusion.81 = f32[4,256,256]{2,1,0:T(8,128)S(1)} fusion(f32[4,256,256]{2,1,0:T(8,128)S(1)} %fusion.79, f32[4,256,256]{2,1,0:T(8,128)S(1)} %fusion.17), kind=kOutput, calls=%fused_computation.160 | convolution fusion | flops 805306368 | bytes 3145728 | tf_op jit(solution)/shard_map/aij,ajk->aik/dot_general | solution.py:34
  66.5 1.1 %fusion.80 = f32[4,256,256]{2,1,0:T(8,128)S(1)} fusion(f32[4,256,256]{2,1,0:T(8,128)S(1)} %fusion.17, f32[4,256,256]{2,1,0:T(8,128)S(1)} %fusion.78), kind=kOutput, calls=%fused_computation.159 | convolution fusion | flops 805306368 | bytes 3145728 | tf_op jit(solution)/shard_map/aij,ajk->aik/dot_general | solution.py:35
  67.9 1.4 %fusion.16 = f32[4,256,256]{2,1,0:T(8,128)S(1)} fusion(f32[4,256,256]{2,1,0:T(8,128)S(1)} %fusion.80, f32[4,256,256]{2,1,0:T(8,128)S(1)} %fusion.81, f32[256,256]{1,0:T(8,128)S(1)} %fusion.53), kind=kOutput, calls=%fused_computation.26 | convolution fusion | flops 805830656 | bytes 3407872 | tf_op jit(solution)/shard_map/aij,ajk->aik/dot_general | solution.py:31
  69.3 1.1 %convolution_divide_fusion = f32[4,256,256]{2,1,0:T(8,128)S(1)} fusion(f32[4,256,256]{2,1,0:T(8,128)S(1)} %fusion.16, f32[4,256,256]{2,1,0:T(8,128)S(1)} %fusion.80, f32[4]{0:T(128)S(1)} %get-tuple-element.21), kind=kOutput, calls=%fused_computation.24 | convolution fusion | flops 805568512 | bytes 3145744 | tf_op jit(solution)/shard_map/aij,ajk->aik/dot_general | solution.py:35
  70.5 1.0 fusion.62
  71.5 1.0 fusion.60
  72.7 2.3 %collective-permute-start = (bf16[1,4,256,256]{3,2,1,0:T(8,128)(2,1)S(1)}, bf16[1,4,256,256]{3,2,1,0:T(8,128)(2,1)S(1)}, u32[]{:S(2)}, u32[]{:S(2)}) collective-permute-start(bf16[1,4,256,256]{3,2,1,0:T(8,128)(2,1)S(1)} %fusion.45), channel_id=1, source_target_pairs={{0,1},{1,2},{2,3},{4,5},{5,6},{6,7},{8,9},{9,10},{10,11},{12,13},{... | collective-permute-start | bytes 1572872 | tf_op jit(solution)/shard_map/ppermute | solution.py:16
  75.0 1.3 %collective-permute-start.1 = (bf16[1,4,256,256]{3,2,1,0:T(8,128)(2,1)S(1)}, bf16[1,4,256,256]{3,2,1,0:T(8,128)(2,1)S(1)}, u32[]{:S(2)}, u32[]{:S(2)}) collective-permute-start(bf16[1,4,256,256]{3,2,1,0:T(8,128)(2,1)S(1)} %fusion.45), channel_id=1, source_target_pairs={{1,0},{2,1},{3,2},{5,4},{6,5},{7,6},{9,8},{10,9},{11,10},{13,12},{... | collective-permute-start | bytes 1572872 | tf_op jit(solution)/shard_map/ppermute | solution.py:19
  77.0 4.1 %all-to-all-start = ((bf16[64,4,512]{2,0,1:T(8,128)(2,1)}), bf16[64,4,512]{2,0,1:T(8,128)(2,1)S(1)}, u32[]{:S(2)}, u32[]{:S(2)}) async-start(bf16[64,4,512]{2,0,1:T(8,128)(2,1)} %bitcast.73), calls=%async_computation | async-start | bytes 524288 | tf_op jit(solution)/shard_map/all_to_all | solution.py:86
  81.7 7.4 %all-to-all-done = bf16[64,4,512]{2,0,1:T(8,128)(2,1)S(1)} async-done(((bf16[64,4,512]{2,0,1:T(8,128)(2,1)}), bf16[64,4,512]{2,0,1:T(8,128)(2,1)S(1)}, u32[]{:S(2)}, u32[]{:S(2)}) %all-to-all-start) | async-done | bytes 262176 | tf_op jit(solution)/shard_map/all_to_all | solution.py:86
  90.7 2.0 %gather_fusion.3 = bf16[16,256,256]{2,1,0:T(8,128)(2,1)} fusion(bf16[12,256,256]{2,1,0:T(8,128)(2,1)S(1)} %bitcast.77, s32[1024]{0:T(1024)S(1)} %pad_clamp_fusion.2), kind=kCustom, calls=%fused_computation.1.clone | custom fusion | bytes 4194368 | tf_op jit(solution)/shard_map/jit(_take)/gather | solution.py:99
  92.7 2.0 %gather_fusion.4 = bf16[16,256,256]{2,1,0:T(8,128)(2,1)} fusion(bf16[12,256,256]{2,1,0:T(8,128)(2,1)S(1)} %bitcast.78, s32[1024]{0:T(1024)S(1)} %pad_clamp_fusion.1), kind=kCustom, calls=%fused_computation.2.clone | custom fusion | bytes 4194368 | tf_op jit(solution)/shard_map/jit(_take)/gather | solution.py:99
  94.7 2.0 %gather_fusion.5 = bf16[16,256,256]{2,1,0:T(8,128)(2,1)} fusion(bf16[12,256,256]{2,1,0:T(8,128)(2,1)S(1)} %bitcast.79, s32[1024]{0:T(1024)S(1)} %pad_clamp_fusion), kind=kCustom, calls=%fused_computation.3.clone | custom fusion | bytes 4194368 | tf_op jit(solution)/shard_map/jit(_take)/gather | solution.py:99
  96.7 2.0 %gather_fusion.2 = bf16[16,256,256]{2,1,0:T(8,128)(2,1)} fusion(bf16[12,256,256]{2,1,0:T(8,128)(2,1)S(1)} %bitcast.80, s32[1024]{0:T(1024)S(1)} %pad_clamp_fusion.3), kind=kCustom, calls=%fused_computation.clone | custom fusion | bytes 4194368 | tf_op jit(solution)/shard_map/jit(_take)/gather | solution.py:99
  98.7 2.3 %fusion.29 = f32[16,32,256]{2,1,0:T(8,128)S(1)} fusion(bf16[256,16,32]{0,2,1:T(8,128)(2,1)S(1)} %subtract_convert_fusion, bf16[16,256,256]{2,1,0:T(8,128)(2,1)} %gather_fusion.3, pred[16]{0:T(512)(128)(4,1)S(1)} %compare_and_fusion.4, f32[16,32]{1,0:T(8,128)S(1)} %mul.175), kind=kOutput, calls=%fused_computation.36 | convolution fusion | flops 68288512 | bytes 2885648 | tf_op jit(solution)/shard_map/kgc,gkj->gcj/dot_general | solution.py:100
  101.5 1.0 copy-done.1
  103.9 0.8 fusion.46
  (68 shorter events, 6.4 us)
Async XLA Ops:
  0.0 6.2 %copy-start.4 = (s32[1,1024]{1,0:T(1,128)S(1)}, s32[1,1024]{1,0:T(1,128)}, u32[]{:S(2)}) copy-start(s32[1,1024]{1,0:T(1,128)} %param.11) | copy-start | bytes 12292
  2.9 45.1 %copy-start.7 = (f32[1,1024]{1,0:T(1,128)S(1)}, f32[1,1024]{1,0:T(1,128)}, u32[]{:S(2)}) copy-start(f32[1,1024]{1,0:T(1,128)} %param.9) | copy-start | bytes 12292
  38.9 17.5 %copy-start.6 = (f32[1,4,1024]{2,1,0:T(4,128)S(1)}, f32[1,4,1024]{2,1,0:T(4,128)}, u32[]{:S(2)}) copy-start(f32[1,4,1024]{2,1,0:T(4,128)} %param.12) | copy-start | bytes 49156
  70.5 5.8 %copy-start.3 = (bf16[64,2048]{1,0:T(8,128)(2,1)S(1)}, bf16[64,2048]{1,0:T(8,128)(2,1)}, u32[]{:S(2)}) copy-start(bf16[64,2048]{1,0:T(8,128)(2,1)} %param.8) | copy-start | bytes 786436
  71.5 9.8 %copy-start.5 = (f32[4,512]{1,0:T(4,128)S(1)}, f32[4,512]{1,0:T(4,128)}, u32[]{:S(2)}) copy-start(f32[4,512]{1,0:T(4,128)} %param.13) | copy-start | bytes 24580
  72.7 17.8 %collective-permute-start = (bf16[1,4,256,256]{3,2,1,0:T(8,128)(2,1)S(1)}, bf16[1,4,256,256]{3,2,1,0:T(8,128)(2,1)S(1)}, u32[]{:S(2)}, u32[]{:S(2)}) collective-permute-start(bf16[1,4,256,256]{3,2,1,0:T(8,128)(2,1)S(1)} %fusion.45), channel_id=1, source_target_pairs={{0,1},{1,2},{2,3},{4,5},{5,6},{6,7},{8,9},{9,10},{10,11},{12,13},{... | collective-permute-start | bytes 1572872 | tf_op jit(solution)/shard_map/ppermute | solution.py:16
  75.0 15.5 %collective-permute-start.1 = (bf16[1,4,256,256]{3,2,1,0:T(8,128)(2,1)S(1)}, bf16[1,4,256,256]{3,2,1,0:T(8,128)(2,1)S(1)}, u32[]{:S(2)}, u32[]{:S(2)}) collective-permute-start(bf16[1,4,256,256]{3,2,1,0:T(8,128)(2,1)S(1)} %fusion.45), channel_id=1, source_target_pairs={{1,0},{2,1},{3,2},{5,4},{6,5},{7,6},{9,8},{10,9},{11,10},{13,12},{... | collective-permute-start | bytes 1572872 | tf_op jit(solution)/shard_map/ppermute | solution.py:19
  77.0 12.1 %all-to-all-start = ((bf16[64,4,512]{2,0,1:T(8,128)(2,1)}), bf16[64,4,512]{2,0,1:T(8,128)(2,1)S(1)}, u32[]{:S(2)}, u32[]{:S(2)}) async-start(bf16[64,4,512]{2,0,1:T(8,128)(2,1)} %bitcast.73), calls=%async_computation | async-start | bytes 524288 | tf_op jit(solution)/shard_map/all_to_all | solution.py:86
  98.7 2.3 %copy-start.2 = (bf16[16,256,256]{2,1,0:T(8,128)(2,1)S(1)}, bf16[16,256,256]{2,1,0:T(8,128)(2,1)}, u32[]{:S(2)}) copy-start(bf16[16,256,256]{2,1,0:T(8,128)(2,1)} %gather_fusion.4) | copy-start | bytes 6291460
  101.0 1.6 %copy-start.1 = (bf16[16,256,256]{2,1,0:T(8,128)(2,1)S(1)}, bf16[16,256,256]{2,1,0:T(8,128)(2,1)}, u32[]{:S(2)}) copy-start(bf16[16,256,256]{2,1,0:T(8,128)(2,1)} %gather_fusion.5) | copy-start | bytes 6291460
  101.5 1.8 %copy-start = (bf16[16,256,256]{2,1,0:T(8,128)(2,1)S(1)}, bf16[16,256,256]{2,1,0:T(8,128)(2,1)}, u32[]{:S(2)}) copy-start(bf16[16,256,256]{2,1,0:T(8,128)(2,1)} %gather_fusion.2) | copy-start | bytes 6291460
where the time goes:
time: 105 us
  blocking collectives  45.6 us (43%)
  matrix products  19.8 us (19%)
  local copies, waits for them, and re-layouts  19.4 us (18%)
  starting transfers between devices  7.71 us (7%)
  waiting for transfers between devices  7.42 us (7%)
  other arithmetic  3.57 us (3%)
  between operations  1.12 us (1%)
    all_gather x1, blocking collectives, per_device(): pieces = lax.all_gather(border, 'region', axis=1, tiled=True)  32.6 us
    gather x4, local copies, waits for them, and re-layouts, per_device(): chosen = jnp.take(stacked, chosen_index, axis=0)  8.04 us
    all_to_all x1, waiting for transfers between devices, per_device(): lax.all_to_all(ensemble, 'member', split_axis=1, concat_axis=0, tiled=True)  7.41 us
    all_gather x1, blocking collectives, per_device(): report_pert = lax.all_gather(local_pert, 'member', axis=0, tiled=True)  7.41 us
    psum x1, blocking collectives, per_device(): report_mean = lax.psum(jnp.sum(at_reports, axis=0), 'member') / members  5.67 us
    dot_general x4, matrix products, make_transform(): jnp.einsum('aij,ajk->aik', root_iter, current, precision=highest)  4.92 us
    dot_general x4, matrix products, make_transform(): root_iter = jnp.einsum('aij,ajk->aik', middle, root_iter, precision=highest)  4.53 us
    all_to_all x1, starting transfers between devices, per_device(): lax.all_to_all(ensemble, 'member', split_axis=1, concat_axis=0, tiled=True)  4.14 us
  transfers between devices with their start and end apart: 3, of which 1 were waited for; matrix products, arithmetic and copies ran while one was open for 2% of the time, Pallas kernels for 0%

commit v1 on v0

--- a/solution.py
+++ b/solution.py
@@ -6,6 +6,13 @@
 MARGIN = 128
 SWEEPS = 4
 highest = lax.Precision.HIGHEST
+
+
+def trade_parts(block, axis, split, join):
+    n_dev = lax.axis_size(axis)
+    tiles = jnp.stack(jnp.split(block, n_dev, axis=split), axis=0)
+    tiles = lax.all_to_all(tiles, axis, split_axis=0, concat_axis=0)
+    return jnp.concatenate(tiles, axis=join)
 
 
 def extended(block, sides, width):
@@ -83,7 +90,7 @@
     slab_cells = cell_count // groups
     group_cells = slab_cells // groups_band
     mixing = blending / jnp.sum(blending, axis=0, keepdims=True)
-    columns = lax.all_to_all(ensemble, "member", split_axis=1, concat_axis=0, tiled=True)
+    columns = trade_parts(ensemble, "member", 1, 0)
     cell_mean = jnp.sum(columns, axis=0, dtype=jnp.float32) / members
     anomaly = (columns - cell_mean[None, :]).astype(jnp.bfloat16)
     anomaly_view = anomaly.reshape(members, groups_band, group_cells)

time: 105 us -> 106 us (level)
  other arithmetic: 3.57 us -> 5.3 us
where the time goes in v1:
time: 106 us
  blocking collectives  45.6 us (43%)
  matrix products  19.8 us (19%)
  local copies, waits for them, and re-layouts  18.6 us (18%)
  starting transfers between devices  7.72 us (7%)
  waiting for transfers between devices  7.38 us (7%)
  other arithmetic  5.3 us (5%)
  between operations  1.12 us (1%)
    all_gather x1, blocking collectives, per_device(): pieces = lax.all_gather(border, 'region', axis=1, tiled=True)  32.6 us
    gather x4, local copies, waits for them, and re-layouts, per_device(): chosen = jnp.take(stacked, chosen_index, axis=0)  8.04 us
    all_gather x1, blocking collectives, per_device(): report_pert = lax.all_gather(local_pert, 'member', axis=0, tiled=True)  7.41 us
    all_to_all x1, waiting for transfers between devices, trade_parts(): tiles = lax.all_to_all(tiles, axis, split_axis=0, concat_axis=0)  7.37 us
    psum x1, blocking collectives, per_device(): report_mean = lax.psum(jnp.sum(at_reports, axis=0), 'member') / members  5.67 us
    dot_general x4, matrix products, make_transform(): jnp.einsum('aij,ajk->aik', root_iter, current, precision=highest)  4.92 us
    dot_general x4, matrix products, make_transform(): root_iter = jnp.einsum('aij,ajk->aik', middle, root_iter, precision=highest)  4.53 us
    all_to_all x1, starting transfers between devices, trade_parts(): tiles = lax.all_to_all(tiles, axis, split_axis=0, concat_axis=0)  4.14 us
  transfers between devices with their start and end apart: 3, of which 1 were waited for; matrix products, arithmetic and copies ran while one was open for 2% of the time, Pallas kernels for 0%

profile of v1, /device:TPU:0, one launch (start us, length us, event | category | flops | bytes accessed | tf_op | source)
XLA Modules:
  0.0 105.6 jit_solution(17278711875546461227)
XLA Ops:
  1.6 1.2 %copy.13 = bf16[64,2048]{0,1:T(8,128)(2,1)S(1)} copy(bf16[64,2048]{1,0:T(8,128)(2,1)} %param.8) | data formatting | bytes 524288 | tf_op args[0]
  2.9 3.2 %gather_fusion = bf16[1024,64]{1,0:T(8,128)(2,1)S(1)} fusion(bf16[64,2048]{0,1:T(8,128)(2,1)S(1)} %copy.13, s32[1024]{0:T(1024)S(1)} %broadcast_clamp_fusion.1), kind=kCustom, calls=%fused_computation.4 | custom fusion | bytes 266240 | tf_op jit(solution)/shard_map/jit(_take)/gather | solution.py:69
  6.3 32.6 %all_gather.6 = bf16[64,1024]{0,1:T(8,128)(2,1)S(1)} all-gather(bf16[64,128]{0,1:T(8,128)(2,1)S(1)} %slice.37), channel_id=1, replica_groups=mesh['region'=8,'member'=4] {'region'}, dimensions={1}, use_global_device_ids=true | all-gather | bytes 147456 | tf_op jit(solution)/shard_map/all_gather | solution.py:72
  38.9 3.2 %gather_fusion.1 = bf16[1024,64]{1,0:T(8,128)(2,1)S(1)} fusion(bf16[64,1024]{0,1:T(8,128)(2,1)S(1)} %all_gather.6, s32[1024]{0:T(1024)S(1)} %broadcast_clamp_fusion), kind=kCustom, calls=%fused_computation.5 | custom fusion | bytes 266240 | tf_op jit(solution)/shard_map/jit(_take)/gather | solution.py:75
  42.3 5.7 %psum.7 = f32[1024]{0:T(1024)S(1)} all-reduce(f32[1024]{0:T(1024)S(1)} %fusion.54), channel_id=1, replica_groups=mesh['region'=8,'member'=4] {'member'}, use_global_device_ids=true, to_apply=%region_3.4 | all-reduce | flops 1024 | bytes 8192 | tf_op jit(solution)/shard_map/psum | solution.py:78
  48.1 7.4 %all_gather.7 = bf16[256,1024]{1,0:T(8,128)(2,1)S(1)} all-gather(bf16[64,1024]{1,0:T(8,128)(2,1)S(1)} %fusion.56), channel_id=1, replica_groups=mesh['region'=8,'member'=4] {'member'}, dimensions={0}, use_global_device_ids=true | all-gather | bytes 655360 | tf_op jit(solution)/shard_map/all_gather | solution.py:80
  56.3 0.9 multiply_reduce_fusion
  57.2 1.2 %fusion.19 = f32[4,256,256]{2,1,0:T(8,128)S(1)} fusion(f32[256,256]{1,0:T(8,128)S(1)} %fusion.52, f32[256,256]{1,0:T(8,128)S(1)} %fusion.53, f32[4,256,256]{2,1,0:T(8,128)S(1)} %get-tuple-element.28, f32[4]{0:T(128)S(1)} %get-tuple-element.26), kind=kOutput, calls=%fused_computation.32 | convolution fusion | flops 806092800 | bytes 2621456 | tf_op jit(solution)/shard_map/aij,ajk->aik/dot_general | solution.py:38
  58.4 1.2 %fusion.55 = f32[4,256,256]{2,1,0:T(8,128)S(1)} fusion(f32[4,256,256]{2,1,0:T(8,128)S(1)} %fusion.19, f32[4,256,256]{2,1,0:T(8,128)S(1)} %get-tuple-element.28, f32[4]{0:T(128)S(1)} %get-tuple-element.26), kind=kOutput, calls=%fused_computation.64 | convolution fusion | flops 805568512 | bytes 3145744 | tf_op jit(solution)/shard_map/aij,ajk->aik/dot_general | solution.py:41
  59.6 1.1 %fusion.48 = f32[4,256,256]{2,1,0:T(8,128)S(1)} fusion(f32[4,256,256]{2,1,0:T(8,128)S(1)} %fusion.19, f32[256,256]{1,0:T(8,128)S(1)} %fusion.52), kind=kOutput, calls=%fused_computation.52 | convolution fusion | flops 805306368 | bytes 2359296 | tf_op jit(solution)/shard_map/aij,ajk->aik/dot_general | solution.py:42
  60.7 1.2 %fusion.18 = f32[4,256,256]{2,1,0:T(8,128)S(1)} fusion(f32[4,256,256]{2,1,0:T(8,128)S(1)} %fusion.48, f32[4,256,256]{2,1,0:T(8,128)S(1)} %fusion.55, f32[256,256]{1,0:T(8,128)S(1)} %fusion.53), kind=kOutput, calls=%fused_computation.30 | convolution fusion | flops 805830656 | bytes 3407872 | tf_op jit(solution)/shard_map/aij,ajk->aik/dot_general | solution.py:38
  61.9 1.1 %fusion.79 = f32[4,256,256]{2,1,0:T(8,128)S(1)} fusion(f32[4,256,256]{2,1,0:T(8,128)S(1)} %fusion.55, f32[4,256,256]{2,1,0:T(8,128)S(1)} %fusion.18), kind=kOutput, calls=%fused_computation.161 | convolution fusion | flops 805306368 | bytes 3145728 | tf_op jit(solution)/shard_map/aij,ajk->aik/dot_general | solution.py:41
  63.0 1.1 %fusion.78 = f32[4,256,256]{2,1,0:T(8,128)S(1)} fusion(f32[4,256,256]{2,1,0:T(8,128)S(1)} %fusion.18, f32[4,256,256]{2,1,0:T(8,128)S(1)} %fusion.48), kind=kOutput, calls=%fused_computation.160 | convolution fusion | flops 805306368 | bytes 3145728 | tf_op jit(solution)/shard_map/aij,ajk->aik/dot_general | solution.py:42
  64.2 1.2 %fusion.17 = f32[4,256,256]{2,1,0:T(8,128)S(1)} fusion(f32[4,256,256]{2,1,0:T(8,128)S(1)} %fusion.78, f32[4,256,256]{2,1,0:T(8,128)S(1)} %fusion.79, f32[256,256]{1,0:T(8,128)S(1)} %fusion.53), kind=kOutput, calls=%fused_computation.28 | convolution fusion | flops 805830656 | bytes 3407872 | tf_op jit(solution)/shard_map/aij,ajk->aik/dot_general | solution.py:38
  65.4 1.1 %fusion.81 = f32[4,256,256]{2,1,0:T(8,128)S(1)} fusion(f32[4,256,256]{2,1,0:T(8,128)S(1)} %fusion.79, f32[4,256,256]{2,1,0:T(8,128)S(1)} %fusion.17), kind=kOutput, calls=%fused_computation.163 | convolution fusion | flops 805306368 | bytes 3145728 | tf_op jit(solution)/shard_map/aij,ajk->aik/dot_general | solution.py:41
  66.5 1.1 %fusion.80 = f32[4,256,256]{2,1,0:T(8,128)S(1)} fusion(f32[4,256,256]{2,1,0:T(8,128)S(1)} %fusion.17, f32[4,256,256]{2,1,0:T(8,128)S(1)} %fusion.78), kind=kOutput, calls=%fused_computation.162 | convolution fusion | flops 805306368 | bytes 3145728 | tf_op jit(solution)/shard_map/aij,ajk->aik/dot_general | solution.py:42
  67.9 1.4 %fusion.16 = f32[4,256,256]{2,1,0:T(8,128)S(1)} fusion(f32[4,256,256]{2,1,0:T(8,128)S(1)} %fusion.80, f32[4,256,256]{2,1,0:T(8,128)S(1)} %fusion.81, f32[256,256]{1,0:T(8,128)S(1)} %fusion.53), kind=kOutput, calls=%fused_computation.26 | convolution fusion | flops 805830656 | bytes 3407872 | tf_op jit(solution)/shard_map/aij,ajk->aik/dot_general | solution.py:38
  69.3 1.1 %convolution_divide_fusion = f32[4,256,256]{2,1,0:T(8,128)S(1)} fusion(f32[4,256,256]{2,1,0:T(8,128)S(1)} %fusion.16, f32[4,256,256]{2,1,0:T(8,128)S(1)} %fusion.80, f32[4]{0:T(128)S(1)} %get-tuple-element.25), kind=kOutput, calls=%fused_computation.24 | convolution fusion | flops 805568512 | bytes 3145744 | tf_op jit(solution)/shard_map/aij,ajk->aik/dot_general | solution.py:42
  70.5 1.0 fusion.62
  71.5 1.0 fusion.60
  72.7 2.3 %collective-permute-start = (bf16[1,4,256,256]{3,2,1,0:T(8,128)(2,1)S(1)}, bf16[1,4,256,256]{3,2,1,0:T(8,128)(2,1)S(1)}, u32[]{:S(2)}, u32[]{:S(2)}) collective-permute-start(bf16[1,4,256,256]{3,2,1,0:T(8,128)(2,1)S(1)} %fusion.45), channel_id=1, source_target_pairs={{0,1},{1,2},{2,3},{4,5},{5,6},{6,7},{8,9},{9,10},{10,11},{12,13},{... | collective-permute-start | bytes 1572872 | tf_op jit(solution)/shard_map/ppermute | solution.py:23
  75.0 1.3 %collective-permute-start.1 = (bf16[1,4,256,256]{3,2,1,0:T(8,128)(2,1)S(1)}, bf16[1,4,256,256]{3,2,1,0:T(8,128)(2,1)}, u32[]{:S(2)}, u32[]{:S(2)}) collective-permute-start(bf16[1,4,256,256]{3,2,1,0:T(8,128)(2,1)S(1)} %fusion.45), channel_id=1, source_target_pairs={{1,0},{2,1},{3,2},{5,4},{6,5},{7,6},{9,8},{10,9},{11,10},{13,12},{... | collective-permute-start | bytes 1572872 | tf_op jit(solution)/shard_map/ppermute | solution.py:26
  77.1 4.1 %all-to-all-start = ((bf16[4,64,512]{2,1,0:T(8,128)(2,1)}), bf16[4,64,512]{2,1,0:T(8,128)(2,1)S(1)}, u32[]{:S(2)}, u32[]{:S(2)}) async-start(bf16[4,64,512]{2,1,0:T(8,128)(2,1)} %pad_maximum_fusion.1), calls=%async_computation | async-start | bytes 524288 | tf_op jit(solution)/shard_map/all_to_all | solution.py:14
  81.7 7.4 %all-to-all-done = bf16[4,64,512]{2,1,0:T(8,128)(2,1)S(1)} async-done(((bf16[4,64,512]{2,1,0:T(8,128)(2,1)}), bf16[4,64,512]{2,1,0:T(8,128)(2,1)S(1)}, u32[]{:S(2)}, u32[]{:S(2)}) %all-to-all-start) | async-done | bytes 262176 | tf_op jit(solution)/shard_map/all_to_all | solution.py:14
  90.3 1.2 %pad_maximum_fusion = bf16[3,4,256,256]{3,2,1,0:T(8,128)(2,1)S(1)} fusion(bf16[1,4,256,256]{3,2,1,0:T(8,128)(2,1)} %collective-permute-done.1, bf16[1,4,256,256]{3,2,1,0:T(8,128)(2,1)S(1)} %fusion.45, bf16[1,4,256,256]{3,2,1,0:T(8,128)(2,1)S(1)} %collective-permute-done), kind=kLoop, calls=%fused_computation.22 | loop fusion | flops 1572864 | bytes 3145728 | tf_op jit(solution)/shard_map/concatenate | solution.py:27
  91.6 2.0 %gather_fusion.4 = bf16[16,256,256]{2,1,0:T(8,128)(2,1)} fusion(bf16[12,256,256]{2,1,0:T(8,128)(2,1)S(1)} %bitcast.79, s32[1024]{0:T(1024)S(1)} %pad_clamp_fusion.1), kind=kCustom, calls=%fused_computation.2.clone | custom fusion | bytes 4194368 | tf_op jit(solution)/shard_map/jit(_take)/gather | solution.py:106
  93.5 2.0 %gather_fusion.3 = bf16[16,256,256]{2,1,0:T(8,128)(2,1)} fusion(bf16[12,256,256]{2,1,0:T(8,128)(2,1)S(1)} %bitcast.80, s32[1024]{0:T(1024)S(1)} %pad_clamp_fusion.2), kind=kCustom, calls=%fused_computation.1.clone | custom fusion | bytes 4194368 | tf_op jit(solution)/shard_map/jit(_take)/gather | solution.py:106
  95.5 2.0 %gather_fusion.5 = bf16[16,256,256]{2,1,0:T(8,128)(2,1)} fusion(bf16[12,256,256]{2,1,0:T(8,128)(2,1)S(1)} %bitcast.81, s32[1024]{0:T(1024)S(1)} %pad_clamp_fusion), kind=kCustom, calls=%fused_computation.3.clone | custom fusion | bytes 4194368 | tf_op jit(solution)/shard_map/jit(_take)/gather | solution.py:106
  97.6 2.0 %gather_fusion.2 = bf16[16,256,256]{2,1,0:T(8,128)(2,1)} fusion(bf16[12,256,256]{2,1,0:T(8,128)(2,1)S(1)} %bitcast.82, s32[1024]{0:T(1024)S(1)} %pad_clamp_fusion.3), kind=kCustom, calls=%fused_computation.clone | custom fusion | bytes 4194368 | tf_op jit(solution)/shard_map/jit(_take)/gather | solution.py:106
  99.6 2.3 %fusion.32 = f32[16,32,256]{2,1,0:T(8,128)S(1)} fusion(bf16[256,16,32]{0,2,1:T(8,128)(2,1)S(1)} %subtract_convert_fusion, bf16[16,256,256]{2,1,0:T(8,128)(2,1)} %gather_fusion.4, pred[16]{0:T(512)(128)(4,1)S(1)} %get-tuple-element.34, f32[16,32]{1,0:T(8,128)S(1)} %mul.178), kind=kOutput, calls=%fused_computation.37 | convolution fusion | flops 68288512 | bytes 2885648 | tf_op jit(solution)/shard_map/kgc,gkj->gcj/dot_general | solution.py:107
  102.4 1.1 copy-done.1
  104.8 0.8 fusion.46
  (68 shorter events, 6.9 us)
Async XLA Ops:
  0.0 6.2 %copy-start.4 = (s32[1,1024]{1,0:T(1,128)S(1)}, s32[1,1024]{1,0:T(1,128)}, u32[]{:S(2)}) copy-start(s32[1,1024]{1,0:T(1,128)} %param.11) | copy-start | bytes 12292
  2.9 45.1 %copy-start.7 = (f32[1,1024]{1,0:T(1,128)S(1)}, f32[1,1024]{1,0:T(1,128)}, u32[]{:S(2)}) copy-start(f32[1,1024]{1,0:T(1,128)} %param.9) | copy-start | bytes 12292
  38.9 17.5 %copy-start.6 = (f32[1,4,1024]{2,1,0:T(4,128)S(1)}, f32[1,4,1024]{2,1,0:T(4,128)}, u32[]{:S(2)}) copy-start(f32[1,4,1024]{2,1,0:T(4,128)} %param.12) | copy-start | bytes 49156
  70.5 5.8 %copy-start.3 = (bf16[64,2048]{1,0:T(8,128)(2,1)S(1)}, bf16[64,2048]{1,0:T(8,128)(2,1)}, u32[]{:S(2)}) copy-start(bf16[64,2048]{1,0:T(8,128)(2,1)} %param.8) | copy-start | bytes 786436
  71.5 9.8 %copy-start.5 = (f32[4,512]{1,0:T(4,128)S(1)}, f32[4,512]{1,0:T(4,128)}, u32[]{:S(2)}) copy-start(f32[4,512]{1,0:T(4,128)} %param.13) | copy-start | bytes 24580
  72.7 17.6 %collective-permute-start = (bf16[1,4,256,256]{3,2,1,0:T(8,128)(2,1)S(1)}, bf16[1,4,256,256]{3,2,1,0:T(8,128)(2,1)S(1)}, u32[]{:S(2)}, u32[]{:S(2)}) collective-permute-start(bf16[1,4,256,256]{3,2,1,0:T(8,128)(2,1)S(1)} %fusion.45), channel_id=1, source_target_pairs={{0,1},{1,2},{2,3},{4,5},{5,6},{6,7},{8,9},{9,10},{10,11},{12,13},{... | collective-permute-start | bytes 1572872 | tf_op jit(solution)/shard_map/ppermute | solution.py:23
  75.0 15.3 %collective-permute-start.1 = (bf16[1,4,256,256]{3,2,1,0:T(8,128)(2,1)S(1)}, bf16[1,4,256,256]{3,2,1,0:T(8,128)(2,1)}, u32[]{:S(2)}, u32[]{:S(2)}) collective-permute-start(bf16[1,4,256,256]{3,2,1,0:T(8,128)(2,1)S(1)} %fusion.45), channel_id=1, source_target_pairs={{1,0},{2,1},{3,2},{5,4},{6,5},{7,6},{9,8},{10,9},{11,10},{13,12},{... | collective-permute-start | bytes 1572872 | tf_op jit(solution)/shard_map/ppermute | solution.py:26
  77.1 12.0 %all-to-all-start = ((bf16[4,64,512]{2,1,0:T(8,128)(2,1)}), bf16[4,64,512]{2,1,0:T(8,128)(2,1)S(1)}, u32[]{:S(2)}, u32[]{:S(2)}) async-start(bf16[4,64,512]{2,1,0:T(8,128)(2,1)} %pad_maximum_fusion.1), calls=%async_computation | async-start | bytes 524288 | tf_op jit(solution)/shard_map/all_to_all | solution.py:14
  99.6 2.3 %copy-start.2 = (bf16[16,256,256]{2,1,0:T(8,128)(2,1)S(1)}, bf16[16,256,256]{2,1,0:T(8,128)(2,1)}, u32[]{:S(2)}) copy-start(bf16[16,256,256]{2,1,0:T(8,128)(2,1)} %gather_fusion.3) | copy-start | bytes 6291460
  101.9 1.6 %copy-start.1 = (bf16[16,256,256]{2,1,0:T(8,128)(2,1)S(1)}, bf16[16,256,256]{2,1,0:T(8,128)(2,1)}, u32[]{:S(2)}) copy-start(bf16[16,256,256]{2,1,0:T(8,128)(2,1)} %gather_fusion.5) | copy-start | bytes 6291460
  102.4 1.8 %copy-start = (bf16[16,256,256]{2,1,0:T(8,128)(2,1)S(1)}, bf16[16,256,256]{2,1,0:T(8,128)(2,1)}, u32[]{:S(2)}) copy-start(bf16[16,256,256]{2,1,0:T(8,128)(2,1)} %gather_fusion.2) | copy-start | bytes 6291460
